TPU v7x, 32 devices: a whole 2x2x4 slice. The times are simulated.
32 devices in a mesh: gx: 4 (over y, core), gy: 4 (over z), gz: 2 (over x).
Axes of the slice: x: 2, y: 2, z: 4, core: 2. Of those that a mesh axis runs over, the one named last changes fastest.
Arguments:
- volume: bfloat16 [32, 32, 8, 32, 128], P('gx', 'gy', 'gz'), may hold values from -6 to 6
- conv_kernel: bfloat16 [3, 3, 3, 32, 64], replicated, may hold values from -0.21875 to 0.21875
- dense_one: bfloat16 [16, 16, 4, 64, 2048], P('gx', None, None, ('gy', 'gz')), may hold values from -0.0234375 to 0.0234375
- dense_two: float32 [2048, 256], replicated, may hold values from -0.125 to 0.125
- dense_three: float32 [256, 4], replicated, may hold values from -0.375 to 0.375
- targets: float32 [4, 128], replicated, may hold values from -3 to 3
Outputs:
- prediction: float32 [4, 128], replicated
- grad_dense_one: bfloat16 [16, 16, 4, 64, 2048], P('gx', None, None, ('gy', 'gz'))
- grad_conv: float32 [3, 3, 3, 32, 64], replicated
- grad_volume: bfloat16 [32, 32, 8, 32, 128], P('gx', 'gy', 'gz')
All inputs are finite; a program needn't handle non-finite values.
Results may differ from a plain program's by a relative error of at most 0.008.
Values may be sent and summed in bfloat16 or wider, within the bound.
A program may use at most 128 MiB of HBM per device.

v0:
```python
import jax
import jax.numpy as jnp
from jax import lax
from jax.sharding import PartitionSpec as P

loss_scale = 1024.0
leak_slope = 0.3


def with_halo(array, sides, width):
    for axis, dim in sides:
        size, length = (lax.axis_size(axis), array.shape[dim])
        up = [(i, (i + 1) % size) for i in range(size - 1)]
        down = [(j, i) for i, j in up]
        last = lax.slice_in_dim(array, length - width, length, axis=dim)
        initial = lax.slice_in_dim(array, 0, width, axis=dim)
        before = lax.ppermute(last, axis, up)
        after = lax.ppermute(initial, axis, down)
        array = jnp.concatenate([before, array, after], axis=dim)
    return array


def smooth_leaky(values):
    return leak_slope * values + (1.0 - leak_slope) * jax.nn.softplus(values)


def leaky_derivative(values):
    return leak_slope + (1.0 - leak_slope) * jax.nn.sigmoid(values)


def conv_forward(padded, kernel):
    return lax.conv_general_dilated(
        padded,
        kernel,
        (1, 1, 1),
        "VALID",
        dimension_numbers=("DHWCN", "DHWIO", "DHWCN"),
        preferred_element_type=jnp.float32,
    )


def conv_back_input(padded_grad, kernel):
    flipped = kernel[::-1, ::-1, ::-1]
    return lax.conv_general_dilated(
        padded_grad,
        flipped,
        (1, 1, 1),
        "VALID",
        dimension_numbers=("DHWCN", "DHWOI", "DHWCN"),
        preferred_element_type=jnp.float32,
    )


def conv_back_kernel(padded, gradient):
    return lax.conv_general_dilated(
        padded,
        gradient,
        (1, 1, 1),
        "VALID",
        dimension_numbers=("DHWNC", "DHWOI", "DHWNC"),
        preferred_element_type=jnp.float32,
    )


def pooling(values):
    extent_x, extent_y, extent_z, channels, samples = values.shape
    return values.reshape(
        extent_x // 2, 2, extent_y // 2, 2, extent_z // 2, 2, channels, samples
    ).mean(axis=(1, 3, 5))


def spread(values):
    extent_x, extent_y, extent_z, channels, samples = values.shape
    widened = jnp.broadcast_to(
        values[:, None, :, None, :, None],
        (extent_x, 2, extent_y, 2, extent_z, 2, channels, samples),
    )
    return widened.reshape(2 * extent_x, 2 * extent_y, 2 * extent_z, channels, samples)


def body(volume, conv_kernel, dense_one, dense_two, dense_three, targets):
    padded = with_halo(volume, (("gx", 0), ("gy", 1), ("gz", 2)), 1)
    conv_out = conv_forward(padded, conv_kernel)
    pooled = pooling(smooth_leaky(conv_out)).astype(jnp.bfloat16)
    half_x, half_y, half_z, channels, samples = pooled.shape
    groups_y = lax.axis_size("gy")
    groups_z = lax.axis_size("gz")
    per_group = channels // (groups_y * groups_z)
    arrived = lax.all_to_all(pooled[None], ("gy", "gz"), split_axis=4, concat_axis=0, tiled=True)
    arrived = arrived.reshape(groups_y, groups_z, half_x, half_y, half_z, per_group, samples)
    weights_local = dense_one.reshape(
        half_x, groups_y, half_y, groups_z, half_z, per_group, dense_one.shape[4]
    )
    partial_one = jnp.einsum(
        "uvxyzcb,xuyvzch->hb", arrived, weights_local, preferred_element_type=jnp.float32
    )
    pre_one = lax.psum(partial_one, ("gx", "gy", "gz"))
    hidden_one = smooth_leaky(pre_one)
    pre_two = jnp.dot(dense_two.T, hidden_one, precision=lax.Precision.HIGHEST)
    hidden_two = smooth_leaky(pre_two)
    prediction = jnp.dot(dense_three.T, hidden_two, precision=lax.Precision.HIGHEST)
    error_grad = loss_scale * (prediction - targets)
    grad_pre_two = jnp.dot(
        dense_three, error_grad, precision=lax.Precision.HIGHEST
    ) * leaky_derivative(pre_two)
    grad_pre_one = (
        jnp.dot(dense_two, grad_pre_two, precision=lax.Precision.HIGHEST)
        * leaky_derivative(pre_one)
    ).astype(jnp.bfloat16)
    grad_local = jnp.einsum(
        "uvxyzcb,hb->xuyvzch", arrived, grad_pre_one, preferred_element_type=jnp.float32
    )
    grad_dense_one = (grad_local / samples).astype(jnp.bfloat16).reshape(dense_one.shape)
    grad_arrived = jnp.einsum(
        "xuyvzch,hb->uvxyzcb", weights_local, grad_pre_one, preferred_element_type=jnp.float32
    ).astype(jnp.bfloat16)
    outgoing = grad_arrived.reshape(groups_y * groups_z, half_x, half_y, half_z, per_group, samples)
    returned = lax.all_to_all(outgoing, ("gy", "gz"), split_axis=0, concat_axis=4, tiled=True)
    grad_pooled = returned.reshape(half_x, half_y, half_z, channels, samples)
    grad_out = (spread(grad_pooled.astype(jnp.float32)) / 8.0 * leaky_derivative(conv_out)).astype(
        jnp.bfloat16
    )
    grad_padded = with_halo(grad_out, (("gx", 0), ("gy", 1), ("gz", 2)), 1)
    grad_volume = conv_back_input(grad_padded, conv_kernel).astype(jnp.bfloat16)
    kernel_local = conv_back_kernel(padded, grad_out)
    grad_conv = lax.psum(kernel_local, ("gx", "gy", "gz")) / samples
    return (prediction, grad_dense_one, grad_conv, grad_volume)


def solution(mesh):
    return jax.shard_map(
        body,
        mesh=mesh,
        in_specs=(
            P("gx", "gy", "gz", None, None),
            P(),
            P("gx", None, None, ("gy", "gz"), None),
            P(),
            P(),
            P(),
        ),
        out_specs=(
            P(),
            P("gx", None, None, ("gy", "gz"), None),
            P(),
            P("gx", "gy", "gz", None, None),
        ),
        check_vma=False,
    )
```

profile of v0, /device:TPU:0, one launch (start us, length us, event | category | flops | bytes accessed | tf_op | source)
XLA Modules:
  0.0 460.8 jit_solution(831587311891006706)
XLA Ops:
  7.2 0.0 copy-start
  7.2 0.0 all-reduce.3.cloned.1.call-start
  7.2 1.2 fusion.72
  8.4 2.4 collective-permute-start
  10.9 1.3 collective-permute-start.1
  12.2 0.0 collective-permute-done
  12.2 0.0 copy-start.16
  12.2 2.4 constant_dynamic-update-slice_fusion.1
  14.6 1.8 collective-permute-done.1
  16.5 0.1 fusion.71
  16.5 3.5 collective-permute-start.2
  20.0 1.3 collective-permute-start.3
  21.3 3.3 collective-permute-done.2
  24.6 4.4 collective-permute-done.3
  29.0 0.2 pad_maximum_fusion.8
  29.2 3.4 collective-permute-start.4
  32.7 1.3 collective-permute-start.5
  34.0 14.9 %collective-permute-done.4 = bf16[10,10,1,32,128]{4,3,2,1,0:T(8,128)(2,1)S(1)} collective-permute-done((bf16[10,10,1,32,128]{4,3,2,1,0:T(8,128)(2,1)S(1)}, bf16[10,10,1,32,128]{4,3,2,1,0:T(8,128)(2,1)S(1)}, u32[]{:S(2)}, u32[]{:S(2)}) %collective-permute-start.4) | collective-permute-done | bytes 819232 | tf_op jit(solution)/shard_map/ppermute | solution.py:17
  48.9 4.7 %collective-permute-done.5 = bf16[10,10,1,32,128]{4,3,2,1,0:T(8,128)(2,1)S(1)} collective-permute-done((bf16[10,10,1,32,128]{4,3,2,1,0:T(8,128)(2,1)S(1)}, bf16[10,10,1,32,128]{4,3,2,1,0:T(8,128)(2,1)S(1)}, u32[]{:S(2)}, u32[]{:S(2)}) %collective-permute-start.5) | collective-permute-done | bytes 819232 | tf_op jit(solution)/shard_map/ppermute | solution.py:18
  53.6 18.1 %fusion.16 = (f32[8,8,4,64,128]{4,3,2,1,0:T(8,128)}, f32[8,8,4,64,128]{4,3,2,1,0:T(8,128)}) fusion(bf16[3,3,3,32,64]{4,3,2,1,0:T(8,128)(2,1)S(1)} %copy-done.16, bf16[10,10,1,32,128]{4,3,2,1,0:T(8,128)(2,1)S(1)} %collective-permute-done.5, bf16[10,1,4,32,128]{4,3,2,1,0:T(8,128)(2,1)S(1)} %collective-permute-done.3, ...), kind=kOutput, calls=%fused_computation.18 | convolution fusion | flops 3652583424 | bytes 21803008 | tf_op jit(solution)/shard_map/conv_general_dilated | solution.py:32
  71.7 4.4 reduce_sum.9
  76.1 0.1 fusion.40
  76.2 0.5 copy.34
  76.8 18.9 %all_to_all.24 = bf16[1,4,4,2,64,128]{5,3,2,1,0,4:T(2,128)(2,1)S(1)} all-to-all(bf16[1,4,4,2,64,128]{5,3,2,1,0,4:T(2,128)(2,1)S(1)} %copy.34), channel_id=1, replica_groups=mesh['gx'=4,'gy'=4,'gz'=2] {'gy','gz'}, dimensions={4} | all-to-all | bytes 1048576 | tf_op jit(solution)/shard_map/all_to_all | solution.py:89
  95.7 0.2 copy.54
  95.9 0.1 copy.36
  96.1 0.8 copy-done.8
  96.9 5.7 %fusion.19 = f32[2048,128]{0,1:T(8,128)} fusion(bf16[4,2,4,4,2,8,128]{6,5,4,3,2,1,0:T(8,128)(2,1)S(1)} %bitcast.71, bf16[4,4,4,2,2,8,2048]{6,5,4,3,2,1,0:T(8,128)(2,1)} %bitcast.63), kind=kOutput, calls=%fused_computation.24 | convolution fusion | flops 1073741824 | bytes 9961472 | tf_op jit(solution)/shard_map/uvxyzcb,xuyvzch->hb/dot_general | solution.py:94
  102.6 0.0 all-reduce.3.cloned.1.call-update
  102.6 0.2 all-reduce.5.cloned.1.call-start
  102.8 129.3 %all-reduce.3.cloned.1.call-done = f32[2048,128]{0,1:T(8,128)} async-done(((f32[2048,128]{0,1:T(8,128)}), f32[2048,128]{0,1:T(8,128)}) %all-reduce.3.cloned.1.call-update) | async-done | bytes 1048592 | tf_op jit(solution)/shard_map/psum | solution.py:97
  232.2 3.0 convolution_bitcast_fusion.2
  235.1 0.3 convolution_bitcast_fusion.3
  235.4 0.4 fusion.29
  235.8 3.5 fusion.24
  239.3 0.0 copy-start.6
  239.4 5.9 %fusion.28 = bf16[4,2,4,4,2,8,128]{6,5,4,1,3,0,2:T(8,128)(2,1)S(1)} fusion(bf16[2048,128,1,1,1,1,1]{0,1,6,5,4,3,2:T(8,128)(2,1)S(1)} %fusion.24, bf16[4,4,4,2,2,8,2048]{6,5,4,3,2,1,0:T(8,128)(2,1)} %bitcast.64), kind=kOutput, calls=%fused_computation.36 | convolution fusion | flops 1074003968 | bytes 9437184 | tf_op jit(solution)/shard_map/xuyvzch,hb->uvxyzcb/dot_general | solution.py:114
  245.3 0.1 copy.41
  245.4 0.0 slice-start.1
  245.4 17.2 %all_to_all.25 = bf16[8,4,4,2,8,128]{5,4,3,2,1,0:T(8,128)(2,1)S(1)} all-to-all(bf16[8,4,4,2,8,128]{5,4,3,2,1,0:T(8,128)(2,1)S(1)} %bitcast.70), channel_id=1, replica_groups=mesh['gx'=4,'gy'=4,'gz'=2] {'gy','gz'}, dimensions={0} | all-to-all | bytes 1048576 | tf_op jit(solution)/shard_map/all_to_all | solution.py:118
  262.7 0.1 copy_bitcast_fusion
  262.8 1.1 broadcast_in_dim.2
  263.9 2.9 multiply_convert_fusion.1
  266.8 0.0 copy-start.11
  266.8 0.1 fusion.70
  266.9 1.6 collective-permute-start.6
  268.5 1.6 collective-permute-start.7
  270.0 3.9 collective-permute-done.7
  273.9 0.2 pad_maximum_fusion.11
  274.1 3.1 collective-permute-start.8
  277.2 1.5 collective-permute-start.9
  278.7 15.5 %fusion.68 = f32[3,3,3,32,64]{4,3,2,1,0:T(8,128)} fusion(bf16[8,8,4,64,128]{4,3,2,1,0:T(8,128)(2,1)S(1)} %multiply_convert_fusion.1, bf16[10,10,1,32,128]{4,3,2,1,0:T(8,128)(2,1)S(1)} %copy-done.15, bf16[10,1,4,32,128]{4,3,2,1,0:T(8,128)(2,1)S(1)} %copy-done.11, bf16[10,8,4,32,128]{4,3,2,1,0:T(8,128)(2,1)S(1)} %copy-done.4, ...), kind=kOutput, calls=%fused_computation.92 | convolution fusion | flops 3633709056 | bytes 9330688 | tf_op jit(solution)/shard_map/conv_general_dilated | solution.py:55
  294.2 0.0 all-reduce.5.cloned.1.call-update
  294.2 0.0 copy-start.7
  294.3 0.8 copy-done.5
  295.1 3.0 pad_maximum_fusion.5
  298.1 3.3 collective-permute-start.10
  301.5 1.5 collective-permute-start.11
  303.0 5.6 %fusion.14 = bf16[4,4,4,2,2,8,2048]{6,5,4,2,0,3,1:T(8,128)(2,1)} fusion(bf16[2048,128,1,1,1,1,1]{0,1,6,5,4,3,2:T(8,128)(2,1)S(1)} %copy-done.7, bf16[4,2,4,4,2,8,128]{6,5,4,3,2,1,0:T(8,128)(2,1)S(1)} %bitcast.72), kind=kOutput, calls=%fused_computation.16 | convolution fusion | flops 1082130432 | bytes 9437184 | tf_op jit(solution)/shard_map/uvxyzcb,hb->xuyvzch/dot_general | solution.py:110
  308.7 8.5 %copy.39 = bf16[4,4,4,2,2,8,2048]{6,5,4,3,2,1,0:T(8,128)(2,1)} copy(bf16[4,4,4,2,2,8,2048]{6,5,4,2,0,3,1:T(8,128)(2,1)} %fusion.14) | data formatting | bytes 16777216 | tf_op jit(solution)/shard_map/convert_element_type | solution.py:113
  317.2 111.4 %all-reduce.5.cloned.1.call-done = f32[3,3,3,32,64]{4,3,2,1,0:T(8,128)} async-done(((f32[3,3,3,32,64]{4,3,2,1,0:T(8,128)}), f32[3,3,3,32,64]{4,3,2,1,0:T(8,128)}) %all-reduce.5.cloned.1.call-update) | async-done | bytes 221200 | tf_op jit(solution)/shard_map/psum | solution.py:126
  428.6 1.8 broadcast_multiply_fusion
  430.4 0.0 copy-start.1
  430.5 23.1 %fusion.25 = bf16[8,8,4,32,128]{4,3,2,1,0:T(8,128)(2,1)} fusion(bf16[3,3,3,32,64]{4,3,2,1,0:T(8,128)(2,1)S(1)} %copy-done.17, bf16[10,10,1,64,128]{4,3,2,1,0:T(8,128)(2,1)} %collective-permute-done.11, bf16[10,1,4,64,128]{4,3,2,1,0:T(8,128)(2,1)} %collective-permute-done.9, bf16[1,8,4,64,128]{4,3,2,1,0:T(8,128)(2,1)S(1)} %collective-permute-done.7, ...), kind=kOutput, calls=%fused_computation.29 | convolution fusion | flops 3654418432 | bytes 12038144 | tf_op jit(solution)/shard_map/conv_general_dilated | solution.py:44
  (45 shorter events, 0.1 us)
Async XLA Ops:
  7.2 225.0 %copy-start = (f32[2048,256]{1,0:T(8,128)S(1)}, f32[2048,256]{1,0:T(8,128)}, u32[]{:S(2)}) copy-start(f32[2048,256]{1,0:T(8,128)} %param.9) | copy-start | bytes 6291460
  7.2 225.0 %all-reduce.3.cloned.1.call-start = ((), (), s32[]{:S(2)}) async-start(), calls=%async_computation.2 | async-start | bytes 2097152 | tf_op jit(solution)/shard_map/psum | solution.py:97
  8.4 3.7 collective-permute-start
  10.9 5.5 %collective-permute-start.1 = (bf16[1,8,4,32,128]{4,3,2,1,0:T(8,128)(2,1)S(1)}, bf16[1,8,4,32,128]{4,3,2,1,0:T(8,128)(2,1)S(1)}, u32[]{:S(2)}, u32[]{:S(2)}) collective-permute-start(bf16[1,8,4,32,128]{4,3,2,1,0:T(8,128)(2,1)S(1)} %get-tuple-element.14), channel_id=1, source_target_pairs={{8,0},{16,8},{24,16},{9,1},{17,9},{25,17},{10,2},{18,10},{26,18},{... | collective-permute-start | bytes 786440 | tf_op jit(solution)/shard_map/ppermute | solution.py:18
  12.2 41.4 %copy-start.16 = (bf16[3,3,3,32,64]{4,3,2,1,0:T(8,128)(2,1)S(1)}, bf16[3,3,3,32,64]{4,3,2,1,0:T(8,128)(2,1)}, u32[]{:S(2)}) copy-start(bf16[3,3,3,32,64]{4,3,2,1,0:T(8,128)(2,1)} %param.7) | copy-start | bytes 331780
  16.4 55.2 %copy-start.3 = (bf16[10,8,4,32,128]{4,3,2,1,0:T(8,128)(2,1)}, bf16[10,8,4,32,128]{4,3,2,1,0:T(8,128)(2,1)S(1)}, u32[]{:S(2)}) copy-start(bf16[10,8,4,32,128]{4,3,2,1,0:T(8,128)(2,1)S(1)} %constant_dynamic-update-slice_fusion) | copy-start | bytes 7864324
  16.5 8.1 %collective-permute-start.2 = (bf16[10,1,4,32,128]{4,3,2,1,0:T(8,128)(2,1)S(1)}, bf16[10,1,4,32,128]{4,3,2,1,0:T(8,128)(2,1)S(1)}, u32[]{:S(2)}, u32[]{:S(2)}) collective-permute-start(bf16[10,1,4,32,128]{4,3,2,1,0:T(8,128)(2,1)S(1)} %get-tuple-element.12), channel_id=1, source_target_pairs={{0,2},{2,4},{4,6},{1,3},{3,5},{5,7},{8,10},{10,12},{12,14},{9,11},... | collective-permute-start | bytes 983048 | tf_op jit(solution)/shard_map/ppermute | solution.py:17
  20.0 9.0 %collective-permute-start.3 = (bf16[10,1,4,32,128]{4,3,2,1,0:T(8,128)(2,1)S(1)}, bf16[10,1,4,32,128]{4,3,2,1,0:T(8,128)(2,1)S(1)}, u32[]{:S(2)}, u32[]{:S(2)}) collective-permute-start(bf16[10,1,4,32,128]{4,3,2,1,0:T(8,128)(2,1)S(1)} %get-tuple-element.13), channel_id=1, source_target_pairs={{2,0},{4,2},{6,4},{3,1},{5,3},{7,5},{10,8},{12,10},{14,12},{11,9},... | collective-permute-start | bytes 983048 | tf_op jit(solution)/shard_map/ppermute | solution.py:18
  29.0 42.7 %copy-start.10 = (bf16[10,1,4,32,128]{4,3,2,1,0:T(8,128)(2,1)}, bf16[10,1,4,32,128]{4,3,2,1,0:T(8,128)(2,1)S(1)}, u32[]{:S(2)}) copy-start(bf16[10,1,4,32,128]{4,3,2,1,0:T(8,128)(2,1)S(1)} %collective-permute-done.3) | copy-start | bytes 983044
  29.2 19.7 %collective-permute-start.4 = (bf16[10,10,1,32,128]{4,3,2,1,0:T(8,128)(2,1)S(1)}, bf16[10,10,1,32,128]{4,3,2,1,0:T(8,128)(2,1)S(1)}, u32[]{:S(2)}, u32[]{:S(2)}) collective-permute-start(bf16[10,10,1,32,128]{4,3,2,1,0:T(8,128)(2,1)S(1)} %get-tuple-element.10), channel_id=1, source_target_pairs={{0,1},{2,3},{4,5},{6,7},{8,9},{10,11},{12,13},{14,15},{16,17},{18,... | collective-permute-start | bytes 2457608 | tf_op jit(solution)/shard_map/ppermute | solution.py:17
  32.7 20.9 %collective-permute-start.5 = (bf16[10,10,1,32,128]{4,3,2,1,0:T(8,128)(2,1)S(1)}, bf16[10,10,1,32,128]{4,3,2,1,0:T(8,128)(2,1)S(1)}, u32[]{:S(2)}, u32[]{:S(2)}) collective-permute-start(bf16[10,10,1,32,128]{4,3,2,1,0:T(8,128)(2,1)S(1)} %get-tuple-element.11), channel_id=1, source_target_pairs={{1,0},{3,2},{5,4},{7,6},{9,8},{11,10},{13,12},{15,14},{17,16},{19,... | collective-permute-start | bytes 2457608 | tf_op jit(solution)/shard_map/ppermute | solution.py:18
  48.9 22.8 %copy-start.12 = (bf16[10,10,1,32,128]{4,3,2,1,0:T(8,128)(2,1)}, bf16[10,10,1,32,128]{4,3,2,1,0:T(8,128)(2,1)S(1)}, u32[]{:S(2)}) copy-start(bf16[10,10,1,32,128]{4,3,2,1,0:T(8,128)(2,1)S(1)} %collective-permute-done.4) | copy-start | bytes 2457604
  53.6 18.1 %copy-start.14 = (bf16[10,10,1,32,128]{4,3,2,1,0:T(8,128)(2,1)}, bf16[10,10,1,32,128]{4,3,2,1,0:T(8,128)(2,1)S(1)}, u32[]{:S(2)}) copy-start(bf16[10,10,1,32,128]{4,3,2,1,0:T(8,128)(2,1)S(1)} %collective-permute-done.5) | copy-start | bytes 2457604
  96.0 0.8 copy-start.8
  96.9 138.3 %copy-start.18 = (f32[256,4]{0,1:T(4,128)S(1)}, f32[256,4]{0,1:T(4,128)}, u32[]{:S(2)}) copy-start(f32[256,4]{0,1:T(4,128)} %param.10) | copy-start | bytes 12292
  96.9 138.5 %copy-start.19 = (f32[4,128]{1,0:T(4,128)S(1)}, f32[4,128]{1,0:T(4,128)}, u32[]{:S(2)}) copy-start(f32[4,128]{1,0:T(4,128)} %param.11) | copy-start | bytes 6148
  102.6 326.0 %all-reduce.5.cloned.1.call-start = ((), (), s32[]{:S(2)}) async-start(), calls=%async_computation.3 | async-start | bytes 884736 | tf_op jit(solution)/shard_map/psum | solution.py:126
  235.4 9.9 %copy-start.20 = (f32[4,128]{1,0:T(4,128)}, f32[4,128]{1,0:T(4,128)S(1)}, u32[]{:S(2)}) copy-start(f32[4,128]{1,0:T(4,128)S(1)} %convolution_bitcast_fusion.3) | copy-start | bytes 6148
  239.3 6.0 %copy-start.6 = (bf16[2048,128,1,1,1,1,1]{0,1,6,5,4,3,2:T(8,128)(2,1)}, bf16[2048,128,1,1,1,1,1]{0,1,6,5,4,3,2:T(8,128)(2,1)S(1)}, u32[]{:S(2)}) copy-start(bf16[2048,128,1,1,1,1,1]{0,1,6,5,4,3,2:T(8,128)(2,1)S(1)} %fusion.24) | copy-start | bytes 1572868
  239.4 24.5 %slice-start = ((s8[8388608]{0:T(1024)(128)(4,1)}), s8[4194304]{0:T(1024)(128)(4,1)S(1)}, s32[]{:S(2)}) async-start(s8[8388608]{0:T(1024)(128)(4,1)} %bitcast.66), calls=%async_computation.4 | async-start | bytes 8388608
  245.4 18.5 %slice-start.1 = ((s8[8388608]{0:T(1024)(128)(4,1)}), s8[4194304]{0:T(1024)(128)(4,1)S(1)}, s32[]{:S(2)}) async-start(s8[8388608]{0:T(1024)(128)(4,1)} %bitcast.66), calls=%async_computation.5 | async-start | bytes 8388608
  266.7 12.0 %copy-start.2 = (bf16[8,8,4,64,128]{4,3,2,1,0:T(8,128)(2,1)}, bf16[8,8,4,64,128]{4,3,2,1,0:T(8,128)(2,1)S(1)}, u32[]{:S(2)}) copy-start(bf16[8,8,4,64,128]{4,3,2,1,0:T(8,128)(2,1)S(1)} %multiply_convert_fusion.1) | copy-start | bytes 12582916
  266.7 12.0 %copy-start.4 = (bf16[10,8,4,32,128]{4,3,2,1,0:T(8,128)(2,1)S(1)}, bf16[10,8,4,32,128]{4,3,2,1,0:T(8,128)(2,1)}, u32[]{:S(2)}) copy-start(bf16[10,8,4,32,128]{4,3,2,1,0:T(8,128)(2,1)} %copy-done.3) | copy-start | bytes 7864324
  266.8 12.0 %copy-start.11 = (bf16[10,1,4,32,128]{4,3,2,1,0:T(8,128)(2,1)S(1)}, bf16[10,1,4,32,128]{4,3,2,1,0:T(8,128)(2,1)}, u32[]{:S(2)}) copy-start(bf16[10,1,4,32,128]{4,3,2,1,0:T(8,128)(2,1)} %copy-done.10) | copy-start | bytes 983044
  266.8 12.0 %copy-start.13 = (bf16[10,10,1,32,128]{4,3,2,1,0:T(8,128)(2,1)S(1)}, bf16[10,10,1,32,128]{4,3,2,1,0:T(8,128)(2,1)}, u32[]{:S(2)}) copy-start(bf16[10,10,1,32,128]{4,3,2,1,0:T(8,128)(2,1)} %copy-done.12) | copy-start | bytes 2457604
  266.8 12.0 %copy-start.15 = (bf16[10,10,1,32,128]{4,3,2,1,0:T(8,128)(2,1)S(1)}, bf16[10,10,1,32,128]{4,3,2,1,0:T(8,128)(2,1)}, u32[]{:S(2)}) copy-start(bf16[10,10,1,32,128]{4,3,2,1,0:T(8,128)(2,1)} %copy-done.14) | copy-start | bytes 2457604
  266.9 3.2 collective-permute-start.6
  268.5 5.4 %collective-permute-start.7 = (bf16[1,8,4,64,128]{4,3,2,1,0:T(8,128)(2,1)S(1)}, bf16[1,8,4,64,128]{4,3,2,1,0:T(8,128)(2,1)S(1)}, u32[]{:S(2)}, u32[]{:S(2)}) collective-permute-start(bf16[1,8,4,64,128]{4,3,2,1,0:T(8,128)(2,1)S(1)} %get-tuple-element.9), channel_id=1, source_target_pairs={{8,0},{16,8},{24,16},{9,1},{17,9},{25,17},{10,2},{18,10},{26,18},{... | collective-permute-start | bytes 1572872 | tf_op jit(solution)/shard_map/ppermute | solution.py:18
  274.1 20.2 %collective-permute-start.8 = (bf16[10,1,4,64,128]{4,3,2,1,0:T(8,128)(2,1)S(1)}, bf16[10,1,4,64,128]{4,3,2,1,0:T(8,128)(2,1)S(1)}, u32[]{:S(2)}, u32[]{:S(2)}) collective-permute-start(bf16[10,1,4,64,128]{4,3,2,1,0:T(8,128)(2,1)S(1)} %get-tuple-element.6), channel_id=1, source_target_pairs={{0,2},{2,4},{4,6},{1,3},{3,5},{5,7},{8,10},{10,12},{12,14},{9,11},... | collective-permute-start | bytes 1966088 | tf_op jit(solution)/shard_map/ppermute | solution.py:17
  277.2 17.9 %collective-permute-start.9 = (bf16[10,1,4,64,128]{4,3,2,1,0:T(8,128)(2,1)S(1)}, bf16[10,1,4,64,128]{4,3,2,1,0:T(8,128)(2,1)}, u32[]{:S(2)}, u32[]{:S(2)}) collective-permute-start(bf16[10,1,4,64,128]{4,3,2,1,0:T(8,128)(2,1)S(1)} %get-tuple-element.7), channel_id=1, source_target_pairs={{2,0},{4,2},{6,4},{3,1},{5,3},{7,5},{10,8},{12,10},{14,12},{11,9},... | collective-permute-start | bytes 1966088 | tf_op jit(solution)/shard_map/ppermute | solution.py:18
  294.2 8.8 %copy-start.7 = (bf16[2048,128,1,1,1,1,1]{0,1,6,5,4,3,2:T(8,128)(2,1)S(1)}, bf16[2048,128,1,1,1,1,1]{0,1,6,5,4,3,2:T(8,128)(2,1)}, u32[]{:S(2)}) copy-start(bf16[2048,128,1,1,1,1,1]{0,1,6,5,4,3,2:T(8,128)(2,1)} %copy-done.6) | copy-start | bytes 1572868
  294.3 8.8 %copy-start.9 = (bf16[8,1,4,4,2,8,128]{6,5,4,3,2,0,1:T(8,128)(2,1)S(1)}, bf16[8,1,4,4,2,8,128]{6,5,4,3,2,0,1:T(8,128)(2,1)}, u32[]{:S(2)}) copy-start(bf16[8,1,4,4,2,8,128]{6,5,4,3,2,0,1:T(8,128)(2,1)} %copy-done.8) | copy-start | bytes 1572868
  294.3 0.8 copy-start.5
  298.1 132.3 %collective-permute-start.10 = (bf16[10,10,1,64,128]{4,3,2,1,0:T(8,128)(2,1)}, bf16[10,10,1,64,128]{4,3,2,1,0:T(8,128)(2,1)}, u32[]{:S(2)}, u32[]{:S(2)}) collective-permute-start(bf16[10,10,1,64,128]{4,3,2,1,0:T(8,128)(2,1)} %get-tuple-element.4), channel_id=1, source_target_pairs={{0,1},{2,3},{4,5},{6,7},{8,9},{10,11},{12,13},{14,15},{16,17},{18,... | collective-permute-start | bytes 4915208 | tf_op jit(solution)/shard_map/ppermute | solution.py:17
  301.5 128.9 %collective-permute-start.11 = (bf16[10,10,1,64,128]{4,3,2,1,0:T(8,128)(2,1)S(1)}, bf16[10,10,1,64,128]{4,3,2,1,0:T(8,128)(2,1)}, u32[]{:S(2)}, u32[]{:S(2)}) collective-permute-start(bf16[10,10,1,64,128]{4,3,2,1,0:T(8,128)(2,1)S(1)} %get-tuple-element.5), channel_id=1, source_target_pairs={{1,0},{3,2},{5,4},{7,6},{9,8},{11,10},{13,12},{15,14},{17,16},{19,... | collective-permute-start | bytes 4915208 | tf_op jit(solution)/shard_map/ppermute | solution.py:18
  308.7 121.7 %copy-start.17 = (bf16[3,3,3,32,64]{4,3,2,1,0:T(8,128)(2,1)S(1)}, bf16[3,3,3,32,64]{4,3,2,1,0:T(8,128)(2,1)}, u32[]{:S(2)}) copy-start(bf16[3,3,3,32,64]{4,3,2,1,0:T(8,128)(2,1)} %param.7) | copy-start | bytes 331780
  430.4 23.1 %copy-start.1 = (f32[2048,256]{1,0:T(8,128)S(1)}, f32[2048,256]{1,0:T(8,128)}, u32[]{:S(2)}) copy-start(f32[2048,256]{1,0:T(8,128)} %param.9) | copy-start | bytes 6291460
Sparse Core Ops, SparseCore 0:
  102.7 129.3 all-reduce.2
  294.4 134.2 all-reduce.4
where the time goes:
time: 470 us; the launch traced here: 461 us
  waiting for transfers between devices  274 us (58%)
  matrix products  81.1 us (17%)
  blocking collectives  36.1 us (8%)
  starting transfers between devices  26.1 us (6%)
  local copies, waits for them, and re-layouts  16.1 us (3%)
  between operations  15 us (3%)
  other arithmetic  12.7 us (3%)
    psum x1, waiting for transfers between devices, body(): pre_one = lax.psum(partial_one, ('gx', 'gy', 'gz'))  129 us
    psum x1, waiting for transfers between devices, body(): grad_conv = lax.psum(kernel_local, ('gx', 'gy', 'gz')) / samples  111 us
    conv_general_dilated x1, matrix products, conv_back_input(): lax.conv_general_dilated(padded_grad, flipped, (1, 1, 1), 'VALID', dimens...  23.1 us
    all_to_all x1, blocking collectives, body(): lax.all_to_all(pooled[None], ('gy', 'gz'), split_axis=4, concat_axis=0, t...  18.9 us
    ppermute x6, waiting for transfers between devices, with_halo(): before = lax.ppermute(last, axis, up)  18.2 us
    conv_general_dilated x1, matrix products, conv_forward(): lax.conv_general_dilated(padded, kernel, (1, 1, 1), 'VALID', dimension_nu...  18.1 us
    ppermute x6, starting transfers between devices, with_halo(): before = lax.ppermute(last, axis, up)  17.4 us
    all_to_all x1, blocking collectives, body(): lax.all_to_all(outgoing, ('gy', 'gz'), split_axis=0, concat_axis=4, tiled...  17.2 us
  transfers between devices with their start and end apart: 14, of which 8 were waited for; matrix products, arithmetic and copies ran while one was open for 8% of the time, Pallas kernels for 0%

commit v1 on v0

--- a/solution.py
+++ b/solution.py
@@ -5,6 +5,20 @@
 
 loss_scale = 1024.0
 leak_slope = 0.3
+everyone = ("gx", "gy", "gz")
+
+
+def summed(terms):
+    devices = lax.axis_size(everyone)
+    rows = terms.reshape(-1, terms.shape[-1])
+    count = rows.shape[0]
+    share = -(-count // (16 * devices)) * 16
+    rows = jnp.pad(rows.astype(jnp.bfloat16), ((0, share * devices - count), (0, 0)))
+    rows = rows.reshape(devices, share, -1)
+    rows = lax.all_to_all(rows, everyone, split_axis=0, concat_axis=0, tiled=True)
+    rows = jnp.sum(rows.astype(jnp.float32), axis=0)
+    rows = lax.all_gather(rows, everyone, axis=0, tiled=True)
+    return rows[:count].reshape(terms.shape)
 
 
 def with_halo(array, sides, width):
@@ -92,27 +106,37 @@
         half_x, groups_y, half_y, groups_z, half_z, per_group, dense_one.shape[4]
     )
     partial_one = jnp.einsum(
-        "uvxyzcb,xuyvzch->hb", arrived, weights_local, preferred_element_type=jnp.float32
+        "uvxyzcb,xuyvzch->bh", arrived, weights_local, preferred_element_type=jnp.float32
     )
-    pre_one = lax.psum(partial_one, ("gx", "gy", "gz"))
+    devices = lax.axis_size(everyone)
+    share = samples // devices
+    terms = partial_one.astype(jnp.bfloat16).reshape(devices, share, partial_one.shape[1])
+    terms = lax.all_to_all(terms, everyone, split_axis=0, concat_axis=0, tiled=True)
+    pre_one = jnp.sum(terms.astype(jnp.float32), axis=0)
     hidden_one = smooth_leaky(pre_one)
-    pre_two = jnp.dot(dense_two.T, hidden_one, precision=lax.Precision.HIGHEST)
+    pre_two = jnp.dot(hidden_one, dense_two, precision=lax.Precision.HIGHEST)
     hidden_two = smooth_leaky(pre_two)
-    prediction = jnp.dot(dense_three.T, hidden_two, precision=lax.Precision.HIGHEST)
-    error_grad = loss_scale * (prediction - targets)
+    prediction = jnp.dot(hidden_two, dense_three, precision=lax.Precision.HIGHEST)
+    own_targets = lax.dynamic_slice_in_dim(
+        targets.T, lax.axis_index(everyone) * share, share, axis=0
+    )
+    error_grad = loss_scale * (prediction - own_targets)
     grad_pre_two = jnp.dot(
-        dense_three, error_grad, precision=lax.Precision.HIGHEST
+        error_grad, dense_three.T, precision=lax.Precision.HIGHEST
     ) * leaky_derivative(pre_two)
     grad_pre_one = (
-        jnp.dot(dense_two, grad_pre_two, precision=lax.Precision.HIGHEST)
+        jnp.dot(grad_pre_two, dense_two.T, precision=lax.Precision.HIGHEST)
         * leaky_derivative(pre_one)
     ).astype(jnp.bfloat16)
+    grad_pre_one = lax.all_gather(grad_pre_one, everyone, axis=0, tiled=False)
+    grad_pre_one = grad_pre_one.reshape(samples, partial_one.shape[1])
+    prediction = lax.all_gather(prediction, everyone, axis=0, tiled=True).T
     grad_local = jnp.einsum(
-        "uvxyzcb,hb->xuyvzch", arrived, grad_pre_one, preferred_element_type=jnp.float32
+        "uvxyzcb,bh->xuyvzch", arrived, grad_pre_one, preferred_element_type=jnp.float32
     )
     grad_dense_one = (grad_local / samples).astype(jnp.bfloat16).reshape(dense_one.shape)
     grad_arrived = jnp.einsum(
-        "xuyvzch,hb->uvxyzcb", weights_local, grad_pre_one, preferred_element_type=jnp.float32
+        "xuyvzch,bh->uvxyzcb", weights_local, grad_pre_one, preferred_element_type=jnp.float32
     ).astype(jnp.bfloat16)
     outgoing = grad_arrived.reshape(groups_y * groups_z, half_x, half_y, half_z, per_group, samples)
     returned = lax.all_to_all(outgoing, ("gy", "gz"), split_axis=0, concat_axis=4, tiled=True)
@@ -123,7 +147,7 @@
     grad_padded = with_halo(grad_out, (("gx", 0), ("gy", 1), ("gz", 2)), 1)
     grad_volume = conv_back_input(grad_padded, conv_kernel).astype(jnp.bfloat16)
     kernel_local = conv_back_kernel(padded, grad_out)
-    grad_conv = lax.psum(kernel_local, ("gx", "gy", "gz")) / samples
+    grad_conv = summed(kernel_local) / samples
     return (prediction, grad_dense_one, grad_conv, grad_volume)
 
 

time: 470 us -> 469 us (level)
  waiting for transfers between devices: 274 us -> 48.9 us
  blocking collectives: 36.1 us -> 260 us
  starting transfers between devices: 26.1 us -> 42.2 us
  between operations: 15 us -> 1.59 us
  matrix products: 81.1 us -> 75.2 us
    psum x2 -> x0, waiting for transfers between devices: 241 us -> none  [the longest x1 129 us: body(): pre_one = lax.psum(partial_one, ('gx', 'gy', 'gz'))]
    all_gather x0 -> x3, blocking collectives: none -> 225 us  [the longest x1 89.3 us: body(): prediction = lax.all_gather(prediction, everyone, axis=0, tiled=True).T]
    all_to_all x0 -> x2, waiting for transfers between devices: none -> 16 us  [the longest x1 16 us: body(): lax.all_to_all(terms, everyone, split_axis=0, concat_axis=0, tiled=True)]
    all_to_all x0 -> x2, starting transfers between devices: none -> 15.1 us  [the longest x1 11.6 us: summed(): lax.all_to_all(rows, everyone, split_axis=0, concat_axis=0, tiled=True)]
    dot_general x7, matrix products: 24.4 us -> 19.3 us  [the longest x1 5.87 us: body(): jnp.einsum('xuyvzch,bh->uvxyzcb', weights_local, grad_pre_one, preferred_...]
  transfers between devices with their start and end apart: 14 -> 14, of which waited for: 8 -> 7; matrix products, arithmetic and copies ran while one was open for 8% -> 8% of each run, Pallas kernels for 0% -> 0%
where the time goes in v1:
time: 469 us; the launch traced here: 460 us
  blocking collectives  260 us (55%)
  matrix products  75.2 us (16%)
  waiting for transfers between devices  48.9 us (10%)
  starting transfers between devices  42.2 us (9%)
  local copies, waits for them, and re-layouts  18.2 us (4%)
  other arithmetic  13.7 us (3%)
    all_gather x1, blocking collectives, body(): prediction = lax.all_gather(prediction, everyone, axis=0, tiled=True).T  89.3 us
    all_gather x1, blocking collectives, summed(): rows = lax.all_gather(rows, everyone, axis=0, tiled=True)  68.9 us
    all_gather x1, blocking collectives, body(): grad_pre_one = lax.all_gather(grad_pre_one, everyone, axis=0, tiled=False)  67.1 us
    conv_general_dilated x1, matrix products, conv_back_input(): lax.conv_general_dilated(padded_grad, flipped, (1, 1, 1), 'VALID', dimens...  23.1 us
    all_to_all x1, blocking collectives, body(): lax.all_to_all(pooled[None], ('gy', 'gz'), split_axis=4, concat_axis=0, t...  18.9 us
    ppermute x6, starting transfers between devices, with_halo(): before = lax.ppermute(last, axis, up)  18.9 us
    ppermute x6, waiting for transfers between devices, with_halo(): before = lax.ppermute(last, axis, up)  18.2 us
    conv_general_dilated x1, matrix products, conv_forward(): lax.conv_general_dilated(padded, kernel, (1, 1, 1), 'VALID', dimension_nu...  18.1 us
  transfers between devices with their start and end apart: 14, of which 7 were waited for; matrix products, arithmetic and copies ran while one was open for 8% of the time, Pallas kernels for 0%

profile of v1, /device:TPU:0, one launch (start us, length us, event | category | flops | bytes accessed | tf_op | source)
XLA Modules:
  0.0 459.9 jit_solution(149770252158850535)
XLA Ops:
  0.6 1.2 fusion.76
  1.9 2.4 collective-permute-start
  4.3 1.3 collective-permute-start.1
  5.6 2.4 constant_dynamic-update-slice_fusion.1
  8.1 1.8 collective-permute-done.1
  9.9 0.1 fusion.75
  9.9 3.5 collective-permute-start.2
  13.5 1.3 collective-permute-start.3
  14.8 3.3 collective-permute-done.2
  18.0 4.4 collective-permute-done.3
  22.4 0.2 pad_maximum_fusion.8
  22.6 3.4 collective-permute-start.4
  26.1 1.3 collective-permute-start.5
  27.4 14.9 %collective-permute-done.4 = bf16[10,10,1,32,128]{4,3,2,1,0:T(8,128)(2,1)S(1)} collective-permute-done((bf16[10,10,1,32,128]{4,3,2,1,0:T(8,128)(2,1)S(1)}, bf16[10,10,1,32,128]{4,3,2,1,0:T(8,128)(2,1)S(1)}, u32[]{:S(2)}, u32[]{:S(2)}) %collective-permute-start.4) | collective-permute-done | bytes 819232 | tf_op jit(solution)/shard_map/ppermute | solution.py:31
  42.3 4.7 %collective-permute-done.5 = bf16[10,10,1,32,128]{4,3,2,1,0:T(8,128)(2,1)S(1)} collective-permute-done((bf16[10,10,1,32,128]{4,3,2,1,0:T(8,128)(2,1)S(1)}, bf16[10,10,1,32,128]{4,3,2,1,0:T(8,128)(2,1)S(1)}, u32[]{:S(2)}, u32[]{:S(2)}) %collective-permute-start.5) | collective-permute-done | bytes 819232 | tf_op jit(solution)/shard_map/ppermute | solution.py:32
  47.0 18.1 %fusion.16 = (f32[8,8,4,64,128]{4,3,2,1,0:T(8,128)}, f32[8,8,4,64,128]{4,3,2,1,0:T(8,128)}) fusion(bf16[3,3,3,32,64]{4,3,2,1,0:T(8,128)(2,1)S(1)} %copy-done.15, bf16[10,10,1,32,128]{4,3,2,1,0:T(8,128)(2,1)S(1)} %collective-permute-done.5, bf16[10,1,4,32,128]{4,3,2,1,0:T(8,128)(2,1)S(1)} %collective-permute-done.3, ...), kind=kOutput, calls=%fused_computation.18 | convolution fusion | flops 3652583424 | bytes 21803008 | tf_op jit(solution)/shard_map/conv_general_dilated | solution.py:46
  65.1 4.4 reduce_sum.27
  69.5 0.1 fusion.31
  69.7 0.5 copy.34
  70.2 18.9 %all_to_all.34 = bf16[1,4,4,2,64,128]{5,3,2,1,0,4:T(2,128)(2,1)S(1)} all-to-all(bf16[1,4,4,2,64,128]{5,3,2,1,0,4:T(2,128)(2,1)S(1)} %copy.34), channel_id=1, replica_groups=mesh['gx'=4,'gy'=4,'gz'=2] {'gy','gz'}, dimensions={4} | all-to-all | bytes 1048576 | tf_op jit(solution)/shard_map/all_to_all | solution.py:103
  89.1 0.2 copy.54
  89.3 0.1 copy.36
  89.5 0.8 copy-done.6
  90.3 4.7 %fusion.22 = bf16[128,2048]{1,0:T(8,128)(2,1)S(1)} fusion(bf16[4,2,4,4,2,8,128]{6,5,4,3,2,1,0:T(8,128)(2,1)S(1)} %bitcast.69, bf16[4,4,4,2,2,8,2048]{6,5,4,3,2,1,0:T(8,128)(2,1)} %bitcast.60), kind=kOutput, calls=%fused_computation.24 | convolution fusion | flops 1074003968 | bytes 9437184 | tf_op jit(solution)/shard_map/uvxyzcb,xuyvzch->bh/dot_general | solution.py:108
  95.0 1.0 reshape.70
  96.0 3.5 all-to-all-start.1
  99.5 0.1 constant_dynamic-slice_fusion
  99.6 0.1 copy.45
  99.7 16.0 %all-to-all-done.1 = bf16[32,4,2048]{2,1,0:T(4,128)(2,1)S(1)} async-done(((bf16[32,4,2048]{2,1,0:T(4,128)(2,1)}), bf16[32,4,2048]{2,1,0:T(4,128)(2,1)S(1)}, u32[]{:S(2)}, u32[]{:S(2)}) %all-to-all-start.1) | async-done | bytes 524320 | tf_op jit(solution)/shard_map/all_to_all | solution.py:114
  115.7 0.2 convert_reduce_fusion
  116.0 1.0 fusion.36
  116.9 0.1 fusion.50
  117.1 0.1 convolution_multiply_fusion.1
  117.2 1.8 fusion.26
  119.0 67.1 %all-gather.2 = bf16[32,4,2048]{2,1,0:T(4,128)(2,1)S(1)} all-gather(bf16[1,4,2048]{2,1,0:T(4,128)(2,1)S(1)} %fusion.26), channel_id=2, replica_groups=mesh['gx'=4,'gy'=4,'gz'=2] {'gx','gy','gz'}, dimensions={0}, use_global_device_ids=true | all-gather | bytes 540672 | tf_op jit(solution)/shard_map/all_gather | solution.py:131
  186.1 0.1 reshape.82
  186.3 5.9 %fusion.30 = bf16[4,2,4,4,2,8,128]{6,5,4,1,3,0,2:T(8,128)(2,1)S(1)} fusion(bf16[4,4,4,2,2,8,2048]{6,5,4,3,2,1,0:T(8,128)(2,1)} %bitcast.61, bf16[128,2048,1,1,1,1,1]{1,0,2,3,4,5,6:T(8,128)(2,1)S(1)} %reshape.82), kind=kOutput, calls=%fused_computation.35 | convolution fusion | flops 1074003968 | bytes 9437184 | tf_op jit(solution)/shard_map/xuyvzch,bh->uvxyzcb/dot_general | solution.py:138
  192.1 0.1 copy.41
  192.2 15.9 %all_to_all.35 = bf16[8,4,4,2,8,128]{5,4,3,2,1,0:T(8,128)(2,1)S(1)} all-to-all(bf16[8,4,4,2,8,128]{5,4,3,2,1,0:T(8,128)(2,1)S(1)} %bitcast.67), channel_id=1, replica_groups=mesh['gx'=4,'gy'=4,'gz'=2] {'gy','gz'}, dimensions={0} | all-to-all | bytes 1048576 | tf_op jit(solution)/shard_map/all_to_all | solution.py:142
  208.1 0.1 copy_bitcast_fusion
  208.2 1.1 broadcast_in_dim.2
  209.3 2.9 multiply_convert_fusion.1
  212.2 0.1 fusion.74
  212.3 1.6 collective-permute-start.6
  213.9 1.6 collective-permute-start.7
  215.4 3.8 collective-permute-done.7
  219.3 1.2 pad_maximum_fusion.11
  220.5 3.0 collective-permute-start.8
  223.6 1.5 collective-permute-start.9
  225.1 14.7 %convolution_convert_fusion.1 = bf16[3,3,3,32,64]{4,3,2,1,0:T(8,128)(2,1)S(1)} fusion(bf16[8,8,4,64,128]{4,3,2,1,0:T(8,128)(2,1)S(1)} %multiply_convert_fusion.1, bf16[10,10,1,32,128]{4,3,2,1,0:T(8,128)(2,1)S(1)} %copy-done.14, bf16[10,1,4,32,128]{4,3,2,1,0:T(8,128)(2,1)S(1)} %copy-done.9, bf16[10,8,4,32,128]{4,3,2,1,0:T(8,128)(2,1)S(1)} %copy-done.4, ...), kind=kOutput, calls=%fused_computation.36 | convolution fusion | flops 3633764352 | bytes 9220096 | tf_op jit(solution)/shard_map/conv_general_dilated | solution.py:69
  239.9 0.8 reshape.84
  240.8 11.6 %all-to-all-start.3 = ((bf16[32,2,1024]{2,1,0:T(2,128)(2,1)}), bf16[32,2,1024]{2,1,0:T(2,128)(2,1)S(1)}, u32[]{:S(2)}, u32[]{:S(2)}) async-start(bf16[32,2,1024]{2,1,0:T(2,128)(2,1)} %reshape.84), calls=%async_computation.3 | async-start | bytes 262144 | tf_op jit(solution)/shard_map/all_to_all | solution.py:18
  252.4 3.6 pad_maximum_fusion.5
  256.1 4.9 %collective-permute-start.10 = (bf16[10,10,1,64,128]{4,3,2,1,0:T(8,128)(2,1)}, bf16[10,10,1,64,128]{4,3,2,1,0:T(8,128)(2,1)}, u32[]{:S(2)}, u32[]{:S(2)}) collective-permute-start(bf16[10,10,1,64,128]{4,3,2,1,0:T(8,128)(2,1)} %get-tuple-element.4), channel_id=1, source_target_pairs={{0,1},{2,3},{4,5},{6,7},{8,9},{10,11},{12,13},{14,15},{16,17},{18,... | collective-permute-start | bytes 4915208 | tf_op jit(solution)/shard_map/ppermute | solution.py:31
  260.9 1.3 collective-permute-start.11
  262.2 5.6 %fusion.14 = bf16[4,4,4,2,2,8,2048]{6,5,4,2,0,3,1:T(8,128)(2,1)} fusion(bf16[4,2,4,4,2,8,128]{6,5,4,3,2,1,0:T(8,128)(2,1)S(1)} %bitcast.70, bf16[128,2048,1,1,1,1,1]{1,0,2,3,4,5,6:T(8,128)(2,1)S(1)} %reshape.82), kind=kOutput, calls=%fused_computation.16 | convolution fusion | flops 1082130432 | bytes 9437184 | tf_op jit(solution)/shard_map/uvxyzcb,bh->xuyvzch/dot_general | solution.py:134
  267.8 89.3 %all-gather.1 = f32[32,4,4]{2,1,0:T(4,128)S(1)} all-gather(f32[1,4,4]{2,1,0:T(4,128)S(1)} %bitcast.74), channel_id=1, replica_groups=mesh['gx'=4,'gy'=4,'gz'=2] {'gx','gy','gz'}, dimensions={0}, use_global_device_ids=true | all-gather | bytes 2112 | tf_op jit(solution)/shard_map/all_gather | solution.py:133
  357.2 0.7 copy.38
  357.8 8.5 %copy.40 = bf16[4,4,4,2,2,8,2048]{6,5,4,3,2,1,0:T(8,128)(2,1)} copy(bf16[4,4,4,2,2,8,2048]{6,5,4,2,0,3,1:T(8,128)(2,1)} %fusion.14) | data formatting | bytes 16777216 | tf_op jit(solution)/shard_map/convert_element_type | solution.py:137
  366.3 0.2 reshape.85
  366.5 0.1 convert_reduce_fusion.1
  366.6 68.9 %all_gather.15 = f32[1024,64]{1,0:T(8,128)S(1)} all-gather(f32[32,64]{1,0:T(8,128)S(1)} %convert_reduce_fusion.1), channel_id=1, replica_groups=mesh['gx'=4,'gy'=4,'gz'=2] {'gx','gy','gz'}, dimensions={0}, use_global_device_ids=true | all-gather | bytes 270336 | tf_op jit(solution)/shard_map/all_gather | solution.py:20
  435.5 0.8 slice_multiply_fusion
  436.3 23.1 %fusion.27 = bf16[8,8,4,32,128]{4,3,2,1,0:T(8,128)(2,1)} fusion(bf16[3,3,3,32,64]{4,3,2,1,0:T(8,128)(2,1)S(1)} %copy-done.16, bf16[10,10,1,64,128]{4,3,2,1,0:T(8,128)(2,1)} %collective-permute-done.11, bf16[10,1,4,64,128]{4,3,2,1,0:T(8,128)(2,1)} %collective-permute-done.9, bf16[1,8,4,64,128]{4,3,2,1,0:T(8,128)(2,1)S(1)} %collective-permute-done.7, ...), kind=kOutput, calls=%fused_computation.28 | convolution fusion | flops 3654418432 | bytes 12038144 | tf_op jit(solution)/shard_map/conv_general_dilated | solution.py:58
  (50 shorter events, 0.2 us)
Async XLA Ops:
  0.6 115.3 %copy-start = (f32[2048,256]{1,0:T(8,128)S(1)}, f32[2048,256]{1,0:T(8,128)}, u32[]{:S(2)}) copy-start(f32[2048,256]{1,0:T(8,128)} %param.9) | copy-start | bytes 6291460
  1.9 3.7 collective-permute-start
  4.3 5.5 %collective-permute-start.1 = (bf16[1,8,4,32,128]{4,3,2,1,0:T(8,128)(2,1)S(1)}, bf16[1,8,4,32,128]{4,3,2,1,0:T(8,128)(2,1)S(1)}, u32[]{:S(2)}, u32[]{:S(2)}) collective-permute-start(bf16[1,8,4,32,128]{4,3,2,1,0:T(8,128)(2,1)S(1)} %get-tuple-element.14), channel_id=1, source_target_pairs={{8,0},{16,8},{24,16},{9,1},{17,9},{25,17},{10,2},{18,10},{26,18},{... | collective-permute-start | bytes 786440 | tf_op jit(solution)/shard_map/ppermute | solution.py:32
  5.6 41.4 %copy-start.15 = (bf16[3,3,3,32,64]{4,3,2,1,0:T(8,128)(2,1)S(1)}, bf16[3,3,3,32,64]{4,3,2,1,0:T(8,128)(2,1)}, u32[]{:S(2)}) copy-start(bf16[3,3,3,32,64]{4,3,2,1,0:T(8,128)(2,1)} %param.7) | copy-start | bytes 331780
  9.9 55.2 %copy-start.3 = (bf16[10,8,4,32,128]{4,3,2,1,0:T(8,128)(2,1)}, bf16[10,8,4,32,128]{4,3,2,1,0:T(8,128)(2,1)S(1)}, u32[]{:S(2)}) copy-start(bf16[10,8,4,32,128]{4,3,2,1,0:T(8,128)(2,1)S(1)} %constant_dynamic-update-slice_fusion) | copy-start | bytes 7864324
  9.9 8.1 %collective-permute-start.2 = (bf16[10,1,4,32,128]{4,3,2,1,0:T(8,128)(2,1)S(1)}, bf16[10,1,4,32,128]{4,3,2,1,0:T(8,128)(2,1)S(1)}, u32[]{:S(2)}, u32[]{:S(2)}) collective-permute-start(bf16[10,1,4,32,128]{4,3,2,1,0:T(8,128)(2,1)S(1)} %get-tuple-element.12), channel_id=1, source_target_pairs={{0,2},{2,4},{4,6},{1,3},{3,5},{5,7},{8,10},{10,12},{12,14},{9,11},... | collective-permute-start | bytes 983048 | tf_op jit(solution)/shard_map/ppermute | solution.py:31
  13.5 9.0 %collective-permute-start.3 = (bf16[10,1,4,32,128]{4,3,2,1,0:T(8,128)(2,1)S(1)}, bf16[10,1,4,32,128]{4,3,2,1,0:T(8,128)(2,1)S(1)}, u32[]{:S(2)}, u32[]{:S(2)}) collective-permute-start(bf16[10,1,4,32,128]{4,3,2,1,0:T(8,128)(2,1)S(1)} %get-tuple-element.13), channel_id=1, source_target_pairs={{2,0},{4,2},{6,4},{3,1},{5,3},{7,5},{10,8},{12,10},{14,12},{11,9},... | collective-permute-start | bytes 983048 | tf_op jit(solution)/shard_map/ppermute | solution.py:32
  22.4 42.7 %copy-start.8 = (bf16[10,1,4,32,128]{4,3,2,1,0:T(8,128)(2,1)}, bf16[10,1,4,32,128]{4,3,2,1,0:T(8,128)(2,1)S(1)}, u32[]{:S(2)}) copy-start(bf16[10,1,4,32,128]{4,3,2,1,0:T(8,128)(2,1)S(1)} %collective-permute-done.3) | copy-start | bytes 983044
  22.6 19.7 %collective-permute-start.4 = (bf16[10,10,1,32,128]{4,3,2,1,0:T(8,128)(2,1)S(1)}, bf16[10,10,1,32,128]{4,3,2,1,0:T(8,128)(2,1)S(1)}, u32[]{:S(2)}, u32[]{:S(2)}) collective-permute-start(bf16[10,10,1,32,128]{4,3,2,1,0:T(8,128)(2,1)S(1)} %get-tuple-element.10), channel_id=1, source_target_pairs={{0,1},{2,3},{4,5},{6,7},{8,9},{10,11},{12,13},{14,15},{16,17},{18,... | collective-permute-start | bytes 2457608 | tf_op jit(solution)/shard_map/ppermute | solution.py:31
  26.1 20.9 %collective-permute-start.5 = (bf16[10,10,1,32,128]{4,3,2,1,0:T(8,128)(2,1)S(1)}, bf16[10,10,1,32,128]{4,3,2,1,0:T(8,128)(2,1)S(1)}, u32[]{:S(2)}, u32[]{:S(2)}) collective-permute-start(bf16[10,10,1,32,128]{4,3,2,1,0:T(8,128)(2,1)S(1)} %get-tuple-element.11), channel_id=1, source_target_pairs={{1,0},{3,2},{5,4},{7,6},{9,8},{11,10},{13,12},{15,14},{17,16},{19,... | collective-permute-start | bytes 2457608 | tf_op jit(solution)/shard_map/ppermute | solution.py:32
  42.3 22.8 %copy-start.11 = (bf16[10,10,1,32,128]{4,3,2,1,0:T(8,128)(2,1)}, bf16[10,10,1,32,128]{4,3,2,1,0:T(8,128)(2,1)S(1)}, u32[]{:S(2)}) copy-start(bf16[10,10,1,32,128]{4,3,2,1,0:T(8,128)(2,1)S(1)} %collective-permute-done.4) | copy-start | bytes 2457604
  47.0 18.1 %copy-start.13 = (bf16[10,10,1,32,128]{4,3,2,1,0:T(8,128)(2,1)}, bf16[10,10,1,32,128]{4,3,2,1,0:T(8,128)(2,1)S(1)}, u32[]{:S(2)}) copy-start(bf16[10,10,1,32,128]{4,3,2,1,0:T(8,128)(2,1)S(1)} %collective-permute-done.5) | copy-start | bytes 2457604
  89.5 0.8 copy-start.6
  90.3 9.2 %copy-start.10 = (f32[4,128]{1,0:T(4,128)S(1)}, f32[4,128]{1,0:T(4,128)}, u32[]{:S(2)}) copy-start(f32[4,128]{1,0:T(4,128)} %param.11) | copy-start | bytes 6148
  90.3 26.6 %copy-start.17 = (f32[256,4]{0,1:T(4,128)S(1)}, f32[256,4]{0,1:T(4,128)}, u32[]{:S(2)}) copy-start(f32[256,4]{0,1:T(4,128)} %param.10) | copy-start | bytes 12292
  96.0 19.7 %all-to-all-start.1 = ((bf16[32,4,2048]{2,1,0:T(4,128)(2,1)}), bf16[32,4,2048]{2,1,0:T(4,128)(2,1)S(1)}, u32[]{:S(2)}, u32[]{:S(2)}) async-start(bf16[32,4,2048]{2,1,0:T(4,128)(2,1)} %reshape.70), calls=%async_computation.1 | async-start | bytes 1048576 | tf_op jit(solution)/shard_map/all_to_all | solution.py:114
  186.3 23.0 %slice-start = ((s8[8388608]{0:T(1024)(128)(4,1)}), s8[4194304]{0:T(1024)(128)(4,1)S(1)}, s32[]{:S(2)}) async-start(s8[8388608]{0:T(1024)(128)(4,1)} %bitcast.63), calls=%async_computation.4 | async-start | bytes 8388608
  192.2 17.1 %slice-start.1 = ((s8[8388608]{0:T(1024)(128)(4,1)}), s8[4194304]{0:T(1024)(128)(4,1)S(1)}, s32[]{:S(2)}) async-start(s8[8388608]{0:T(1024)(128)(4,1)} %bitcast.63), calls=%async_computation.5 | async-start | bytes 8388608
  212.2 27.7 %copy-start.2 = (bf16[8,8,4,64,128]{4,3,2,1,0:T(8,128)(2,1)}, bf16[8,8,4,64,128]{4,3,2,1,0:T(8,128)(2,1)S(1)}, u32[]{:S(2)}) copy-start(bf16[8,8,4,64,128]{4,3,2,1,0:T(8,128)(2,1)S(1)} %multiply_convert_fusion.1) | copy-start | bytes 12582916
  212.2 12.9 %copy-start.4 = (bf16[10,8,4,32,128]{4,3,2,1,0:T(8,128)(2,1)S(1)}, bf16[10,8,4,32,128]{4,3,2,1,0:T(8,128)(2,1)}, u32[]{:S(2)}) copy-start(bf16[10,8,4,32,128]{4,3,2,1,0:T(8,128)(2,1)} %copy-done.3) | copy-start | bytes 7864324
  212.2 12.9 %copy-start.9 = (bf16[10,1,4,32,128]{4,3,2,1,0:T(8,128)(2,1)S(1)}, bf16[10,1,4,32,128]{4,3,2,1,0:T(8,128)(2,1)}, u32[]{:S(2)}) copy-start(bf16[10,1,4,32,128]{4,3,2,1,0:T(8,128)(2,1)} %copy-done.8) | copy-start | bytes 983044
  212.2 12.9 %copy-start.12 = (bf16[10,10,1,32,128]{4,3,2,1,0:T(8,128)(2,1)S(1)}, bf16[10,10,1,32,128]{4,3,2,1,0:T(8,128)(2,1)}, u32[]{:S(2)}) copy-start(bf16[10,10,1,32,128]{4,3,2,1,0:T(8,128)(2,1)} %copy-done.11) | copy-start | bytes 2457604
  212.2 12.9 %copy-start.14 = (bf16[10,10,1,32,128]{4,3,2,1,0:T(8,128)(2,1)S(1)}, bf16[10,10,1,32,128]{4,3,2,1,0:T(8,128)(2,1)}, u32[]{:S(2)}) copy-start(bf16[10,10,1,32,128]{4,3,2,1,0:T(8,128)(2,1)} %copy-done.13) | copy-start | bytes 2457604
  212.3 3.2 collective-permute-start.6
  213.9 5.4 %collective-permute-start.7 = (bf16[1,8,4,64,128]{4,3,2,1,0:T(8,128)(2,1)S(1)}, bf16[1,8,4,64,128]{4,3,2,1,0:T(8,128)(2,1)S(1)}, u32[]{:S(2)}, u32[]{:S(2)}) collective-permute-start(bf16[1,8,4,64,128]{4,3,2,1,0:T(8,128)(2,1)S(1)} %get-tuple-element.9), channel_id=1, source_target_pairs={{8,0},{16,8},{24,16},{9,1},{17,9},{25,17},{10,2},{18,10},{26,18},{... | collective-permute-start | bytes 1572872 | tf_op jit(solution)/shard_map/ppermute | solution.py:32
  220.5 31.9 %collective-permute-start.8 = (bf16[10,1,4,64,128]{4,3,2,1,0:T(8,128)(2,1)}, bf16[10,1,4,64,128]{4,3,2,1,0:T(8,128)(2,1)S(1)}, u32[]{:S(2)}, u32[]{:S(2)}) collective-permute-start(bf16[10,1,4,64,128]{4,3,2,1,0:T(8,128)(2,1)} %get-tuple-element.6), channel_id=1, source_target_pairs={{0,2},{2,4},{4,6},{1,3},{3,5},{5,7},{8,10},{10,12},{12,14},{9,11},... | collective-permute-start | bytes 1966088 | tf_op jit(solution)/shard_map/ppermute | solution.py:31
  223.6 28.8 %collective-permute-start.9 = (bf16[10,1,4,64,128]{4,3,2,1,0:T(8,128)(2,1)}, bf16[10,1,4,64,128]{4,3,2,1,0:T(8,128)(2,1)}, u32[]{:S(2)}, u32[]{:S(2)}) collective-permute-start(bf16[10,1,4,64,128]{4,3,2,1,0:T(8,128)(2,1)} %get-tuple-element.7), channel_id=1, source_target_pairs={{2,0},{4,2},{6,4},{3,1},{5,3},{7,5},{10,8},{12,10},{14,12},{11,9},... | collective-permute-start | bytes 1966088 | tf_op jit(solution)/shard_map/ppermute | solution.py:32
  240.8 125.5 %all-to-all-start.3 = ((bf16[32,2,1024]{2,1,0:T(2,128)(2,1)}), bf16[32,2,1024]{2,1,0:T(2,128)(2,1)S(1)}, u32[]{:S(2)}, u32[]{:S(2)}) async-start(bf16[32,2,1024]{2,1,0:T(2,128)(2,1)} %reshape.84), calls=%async_computation.3 | async-start | bytes 262144 | tf_op jit(solution)/shard_map/all_to_all | solution.py:18
  252.4 9.8 %copy-start.7 = (bf16[8,1,4,4,2,8,128]{6,5,4,3,2,0,1:T(8,128)(2,1)S(1)}, bf16[8,1,4,4,2,8,128]{6,5,4,3,2,0,1:T(8,128)(2,1)}, u32[]{:S(2)}) copy-start(bf16[8,1,4,4,2,8,128]{6,5,4,3,2,0,1:T(8,128)(2,1)} %copy-done.6) | copy-start | bytes 1572868
  252.4 3.7 copy-start.5
  256.1 180.2 %collective-permute-start.10 = (bf16[10,10,1,64,128]{4,3,2,1,0:T(8,128)(2,1)}, bf16[10,10,1,64,128]{4,3,2,1,0:T(8,128)(2,1)}, u32[]{:S(2)}, u32[]{:S(2)}) collective-permute-start(bf16[10,10,1,64,128]{4,3,2,1,0:T(8,128)(2,1)} %get-tuple-element.4), channel_id=1, source_target_pairs={{0,1},{2,3},{4,5},{6,7},{8,9},{10,11},{12,13},{14,15},{16,17},{18,... | collective-permute-start | bytes 4915208 | tf_op jit(solution)/shard_map/ppermute | solution.py:31
  260.9 175.4 %collective-permute-start.11 = (bf16[10,10,1,64,128]{4,3,2,1,0:T(8,128)(2,1)}, bf16[10,10,1,64,128]{4,3,2,1,0:T(8,128)(2,1)}, u32[]{:S(2)}, u32[]{:S(2)}) collective-permute-start(bf16[10,10,1,64,128]{4,3,2,1,0:T(8,128)(2,1)} %get-tuple-element.5), channel_id=1, source_target_pairs={{1,0},{3,2},{5,4},{7,6},{9,8},{11,10},{13,12},{15,14},{17,16},{19,... | collective-permute-start | bytes 4915208 | tf_op jit(solution)/shard_map/ppermute | solution.py:32
  357.8 78.5 %copy-start.16 = (bf16[3,3,3,32,64]{4,3,2,1,0:T(8,128)(2,1)S(1)}, bf16[3,3,3,32,64]{4,3,2,1,0:T(8,128)(2,1)}, u32[]{:S(2)}) copy-start(bf16[3,3,3,32,64]{4,3,2,1,0:T(8,128)(2,1)} %param.7) | copy-start | bytes 331780
  436.3 23.1 %copy-start.1 = (f32[2048,256]{1,0:T(8,128)S(1)}, f32[2048,256]{1,0:T(8,128)}, u32[]{:S(2)}) copy-start(f32[2048,256]{1,0:T(8,128)} %param.9) | copy-start | bytes 6291460
